TPU v7x, 256 devices: a whole 4x4x8 slice. The times are simulated.
256 devices in a mesh: grp: 16 (over z, core), ep: 16 (over y, x).
Axes of the slice: x: 4, y: 4, z: 8, core: 2. Of those that a mesh axis runs over, the one named last changes fastest.
Arguments:
- queries: bfloat16 [1024, 64, 576], P(('grp', 'ep')), may hold values from -75 to 75
- cache: bfloat16 [1024, 256, 576], P(('grp', 'ep')), may hold values from -6 to 6
- lengths: int32 [1024], P(('grp', 'ep')), may hold values from 2 to 256, as said below
- live_rows: int32 [256], P(('grp', 'ep')), may hold values from 1 to 4, as said below
- tokens: bfloat16 [4096, 3584], P(('grp', 'ep')), may hold values from -6 to 6
- ids: int32 [4096, 8], P(('grp', 'ep')), may hold values from 0 to 127, all different within a row; in each aligned block of 16 rows (0 to 15, 16 to 31, ...) at most 2 rows name the same one
- gates: float32 [4096, 8], P(('grp', 'ep')), may hold values from 0.1 to 1
- w_gate: bfloat16 [256, 3584, 512], P(('grp', 'ep')), may hold values from -0.09375 to 0.09375
- w_up: bfloat16 [256, 3584, 512], P(('grp', 'ep')), may hold values from -0.09375 to 0.09375
- w_down: bfloat16 [256, 512, 3584], P(('grp', 'ep')), may hold values from -0.1875 to 0.1875
Outputs:
- context: bfloat16 [1024, 64, 512], P(('grp', 'ep'))
- mixed: bfloat16 [4096, 3584], P(('grp', 'ep'))
Inputs may be any that keep to these rules, and one draw needn't show every extreme that they name: `ids`: each row names 8 different experts; among the rows of one device no expert is named more than 2 times. `lengths`: the first request slot of every device holds 256 positions. `live_rows`: a device's live request slots are its first ones; on a quarter of the grp indices every device holds 2 or fewer, elsewhere exactly 4.
All inputs are finite; a program needn't handle non-finite values.
Results may differ from a plain program's by a relative error of at most 0.012.
Values may be sent and summed in bfloat16 or wider, within the bound.
A program may use at most 128 MiB of HBM per device.

v0:
```python
import jax
import jax.numpy as jnp
from jax import lax
from jax.sharding import PartitionSpec as P

TOPK = 8
LAT = 512
CAP = 2
score_scale = 192.0 ** (-0.5)
neg_large = -1e30


def attend(queries, cache, lengths, live_count):
    scores = (
        jnp.einsum("rhc,rlc->rhl", queries, cache, preferred_element_type=jnp.float32) * score_scale
    )
    positions = lax.broadcasted_iota(jnp.int32, scores.shape, 2)
    inside = positions < lengths[:, None, None]
    masked = jnp.where(inside, scores, neg_large)
    highest = jnp.max(masked, axis=2, keepdims=True)
    powers = jnp.where(inside, jnp.exp(masked - highest), 0.0)
    totals = jnp.sum(powers, axis=2, keepdims=True)
    weights = (powers / totals).astype(jnp.bfloat16)
    context = jnp.einsum(
        "rhl,rlc->rhc", weights, cache[:, :, :LAT], preferred_element_type=jnp.float32
    ).astype(jnp.bfloat16)
    request_slot = lax.broadcasted_iota(jnp.int32, context.shape, 0)
    return jnp.where(request_slot < live_count, context, jnp.zeros_like(context))


def expert_partial(flat_rows, w_gate, w_up, w_down):
    gate_part = jnp.dot(flat_rows, w_gate[0], preferred_element_type=jnp.float32)
    up_part = jnp.dot(flat_rows, w_up[0], preferred_element_type=jnp.float32)
    hidden = (jax.nn.silu(gate_part) * up_part).astype(jnp.bfloat16)
    return jnp.dot(hidden, w_down[0], preferred_element_type=jnp.float32)


def per_device(queries, cache, lengths, live_rows, tokens, ids, gates, w_gate, w_up, w_down):
    context = attend(queries, cache, lengths, live_rows[0])
    group_count = lax.axis_size("grp")
    peer_count = lax.axis_size("ep")
    pair_count = peer_count // 2
    row_count = tokens.shape[0]
    feature = tokens.shape[1]
    expert_slots = group_count * CAP
    slot_count = pair_count * expert_slots
    column_rows = group_count * row_count
    all_tokens = lax.all_gather(tokens, "grp", axis=0, tiled=True)
    all_ids = lax.all_gather(ids, "grp", axis=0, tiled=True)
    all_gates = lax.all_gather(gates, "grp", axis=0, tiled=True)
    my_group = lax.axis_index("grp")
    local = all_ids - pair_count * my_group
    experts = jnp.arange(pair_count, dtype=jnp.int32)
    pick_hot = (local[:, :, None] == experts[None, None, :]).astype(jnp.int32)
    token_hot = jnp.sum(pick_hot, axis=1)
    gate_of = jnp.sum(all_gates[:, :, None] * pick_hot.astype(jnp.float32), axis=1)
    blocks = token_hot.reshape(group_count, row_count, pair_count)
    earlier = (jnp.cumsum(blocks, axis=1) - blocks).reshape(column_rows, pair_count)
    source = jnp.arange(column_rows, dtype=jnp.int32)[:, None] // row_count
    slot_id = experts[None, :] * expert_slots + source * CAP + earlier
    slot_id = jnp.where(token_hot > 0, slot_id, slot_count)
    slots = jnp.arange(slot_count, dtype=jnp.int32)
    match = slot_id[:, :, None] == slots[None, None, :]
    dispatch = jnp.any(match, axis=1).T.astype(jnp.bfloat16)
    combine = jnp.sum(jnp.where(match, gate_of[:, :, None], 0.0), axis=1)
    outgoing = jnp.dot(dispatch, all_tokens, preferred_element_type=jnp.float32).astype(
        jnp.bfloat16
    )
    doubled = jnp.repeat(outgoing.reshape(pair_count, expert_slots, feature), 2, axis=0)
    arriving = lax.all_to_all(doubled, "ep", split_axis=0, concat_axis=0, tiled=True)
    partials = expert_partial(
        arriving.reshape(peer_count * expert_slots, feature), w_gate, w_up, w_down
    ).astype(jnp.bfloat16)
    returned = lax.all_to_all(
        partials.reshape(peer_count, expert_slots, feature),
        "ep",
        split_axis=0,
        concat_axis=0,
        tiled=True,
    )
    expert_out = (
        returned.reshape(pair_count, 2, expert_slots, feature)
        .astype(jnp.float32)
        .sum(axis=1)
        .astype(jnp.bfloat16)
        .reshape(slot_count, feature)
    )
    column_mixed = jnp.dot(
        combine,
        expert_out.astype(jnp.float32),
        precision=lax.Precision.HIGHEST,
        preferred_element_type=jnp.float32,
    )
    mixed = lax.psum_scatter(column_mixed, "grp", scatter_dimension=0, tiled=True)
    return (context, mixed.astype(jnp.bfloat16))


def solution(mesh):
    in_specs = (
        P(("grp", "ep"), None, None),
        P(("grp", "ep"), None, None),
        P(("grp", "ep")),
        P(("grp", "ep")),
        P(("grp", "ep"), None),
        P(("grp", "ep"), None),
        P(("grp", "ep"), None),
        P(("grp", "ep"), None, None),
        P(("grp", "ep"), None, None),
        P(("grp", "ep"), None, None),
    )
    out_specs = (P(("grp", "ep"), None, None), P(("grp", "ep"), None))
    return jax.shard_map(
        per_device, mesh=mesh, in_specs=in_specs, out_specs=out_specs, check_vma=False
    )
```

profile of v0, /device:TPU:6, one launch (start us, length us, event | category | flops | bytes accessed | tf_op | source)
XLA Modules:
  0.0 251.7 jit_solution(4051258885842507781)
XLA Ops:
  7.2 0.0 copy-start
  7.2 0.0 all-gather.4.cloned.1.call-start
  7.2 0.7 all-gather.4.cloned.1.call-update
  7.9 20.4 %all-gather = s32[16,16,8]{1,2,0:T(8,128)S(1)} all-gather(s32[1,16,8]{1,2,0:T(8,128)} %bitcast.51), channel_id=1, replica_groups=mesh['grp'=16,'ep'=16] {'grp'}, dimensions={0}, use_global_device_ids=true | all-gather | bytes 8704 | tf_op jit(solution)/shard_map/all_gather | solution.py:49
  28.3 0.1 reshape.126
  28.4 0.1 reshape.114
  28.5 0.1 copy.31
  28.7 0.7 fusion.30
  29.3 0.1 copy.32
  29.5 0.1 reduce_window_sum.14
  29.6 0.1 add_select_fusion
  29.6 0.1 copy.33
  29.8 0.7 fusion.6
  30.5 21.8 %all-gather.4.cloned.1.call-done = bf16[256,3584]{1,0:T(8,128)(2,1)} async-done(((bf16[16,3584]{1,0:T(8,128)(2,1)}), bf16[256,3584]{1,0:T(8,128)(2,1)}) %all-gather.4.cloned.1.call-update) | async-done | bytes 1835024 | tf_op jit(solution)/shard_map/all_gather | solution.py:48
  52.3 2.2 convolution_convert_fusion.1
  54.5 0.4 broadcast_in_dim.46
  54.9 0.0 copy-start.5
  54.9 50.4 %all_to_all.10 = bf16[16,32,3584]{2,1,0:T(8,128)(2,1)S(1)} all-to-all(bf16[16,32,3584]{2,1,0:T(8,128)(2,1)S(1)} %bitcast.45), channel_id=1, replica_groups=mesh['grp'=16,'ep'=16] {'ep'}, dimensions={0} | all-to-all | bytes 7340032 | tf_op jit(solution)/shard_map/all_to_all | solution.py:70
  105.3 0.0 copy-start.1
  105.3 1.8 copy-done.1
  107.1 0.0 copy-done.5
  107.1 2.0 fusion.4
  109.2 10.0 %convolution_convert_fusion = bf16[512,3584]{1,0:T(8,128)(2,1)} fusion(bf16[1,512,3584]{2,1,0:T(8,128)(2,1)} %param.19, bf16[512,3584]{1,0:T(8,128)(2,1)} %bitcast.50, bf16[1,3584,512]{2,1,0:T(8,128)(2,1)} %param.18, f32[512,512]{1,0:T(8,128)S(1)} %fusion.4), kind=kOutput, calls=%fused_computation.1 | convolution fusion | flops 3761504256 | bytes 15728640 | tf_op jit(solution)/shard_map/dot_general | solution.py:35
  119.2 0.0 copy-start.3
  119.2 7.1 %all-to-all-start.1 = ((bf16[16,32,3584]{2,1,0:T(8,128)(2,1)}), bf16[16,32,3584]{2,1,0:T(8,128)(2,1)}, u32[]{:S(2)}, u32[]{:S(2)}) async-start(bf16[16,32,3584]{2,1,0:T(8,128)(2,1)} %bitcast.48), calls=%async_computation.1 | async-start | bytes 7340032 | tf_op jit(solution)/shard_map/all_to_all | solution.py:74
  126.3 0.0 reduce-scatter.2.cloned.1.call-start
  126.4 0.0 copy-done.3
  126.4 15.6 %all-gather.1 = f32[16,16,8]{1,2,0:T(8,128)S(1)} all-gather(f32[1,16,8]{1,2,0:T(8,128)S(1)} %bitcast.52), channel_id=1, replica_groups=mesh['grp'=16,'ep'=16] {'grp'}, dimensions={0}, use_global_device_ids=true | all-gather | bytes 8704 | tf_op jit(solution)/shard_map/all_gather | solution.py:50
  142.0 0.1 reshape.124
  142.1 0.1 copy.35
  142.2 1.5 select_reduce_fusion
  143.7 33.3 %all-to-all-done.1 = bf16[16,32,3584]{2,1,0:T(8,128)(2,1)} async-done(((bf16[16,32,3584]{2,1,0:T(8,128)(2,1)}), bf16[16,32,3584]{2,1,0:T(8,128)(2,1)}, u32[]{:S(2)}, u32[]{:S(2)}) %all-to-all-start.1) | async-done | bytes 3670048 | tf_op jit(solution)/shard_map/all_to_all | solution.py:74
  176.9 2.8 %bitcast_reduce_fusion = bf16[8,32,3584]{2,1,0:T(8,128)(2,1)S(1)} fusion(bf16[16,32,3584]{2,1,0:T(8,128)(2,1)} %all-to-all-done.1), kind=kLoop, calls=%fused_computation.3 | loop fusion | flops 917504 | bytes 5505024 | tf_op jit(solution)/shard_map/reduce_sum | solution.py:84
  179.7 0.0 copy-start.2
  179.7 0.0 copy-start.4
  179.8 3.5 %fusion.31 = f32[256,3584]{1,0:T(8,128)} fusion(f32[256,256]{1,0:T(8,128)S(1)} %select_reduce_fusion, bf16[256,3584]{1,0:T(8,128)(2,1)S(1)} %bitcast.47), kind=kOutput, calls=%fused_computation.45 | convolution fusion | flops 2818572288 | bytes 5767168 | tf_op jit(solution)/shard_map/dot_general | solution.py:88
  183.2 0.0 reduce-scatter.2.cloned.1.call-update
  183.9 0.0 copy-done
  183.9 0.0 copy-done.2
  183.9 0.0 copy-done.4
  183.9 0.3 fusion.14
  184.3 0.2 fusion.29
  184.5 1.2 fusion.17
  185.8 57.5 %reduce-scatter.2.cloned.1.call-done = f32[16,3584]{1,0:T(8,128)} async-done(((f32[256,3584]{1,0:T(8,128)}), f32[16,3584]{1,0:T(8,128)}) %reduce-scatter.2.cloned.1.call-update) | async-done | bytes 229392 | tf_op jit(solution)/shard_map/reduce_scatter | solution.py:94
  243.3 1.6 convert_element_type.35
  (8 shorter events, 0.1 us)
Async XLA Ops:
  7.2 176.8 %copy-start = (bf16[4,64,576]{2,1,0:T(8,128)(2,1)S(1)}, bf16[4,64,576]{2,1,0:T(8,128)(2,1)}, u32[]{:S(2)}) copy-start(bf16[4,64,576]{2,1,0:T(8,128)(2,1)} %param.10) | copy-start | bytes 884740
  7.2 45.1 %all-gather.4.cloned.1.call-start = ((), (), s32[]{:S(2)}) async-start(), calls=%async_computation.3 | async-start | bytes 1949696 | tf_op jit(solution)/shard_map/all_gather | solution.py:48
  54.9 52.2 %copy-start.5 = (bf16[1,3584,512]{2,1,0:T(8,128)(2,1)S(1)}, bf16[1,3584,512]{2,1,0:T(8,128)(2,1)}, u32[]{:S(2)}) copy-start(bf16[1,3584,512]{2,1,0:T(8,128)(2,1)} %param.17) | copy-start | bytes 11010052
  105.3 1.8 copy-start.1
  119.2 7.2 %copy-start.3 = (f32[16,8]{0,1:T(8,128)S(1)}, f32[16,8]{0,1:T(8,128)}, u32[]{:S(2)}) copy-start(f32[16,8]{0,1:T(8,128)} %param.16) | copy-start | bytes 1540
  119.2 57.7 %all-to-all-start.1 = ((bf16[16,32,3584]{2,1,0:T(8,128)(2,1)}), bf16[16,32,3584]{2,1,0:T(8,128)(2,1)}, u32[]{:S(2)}, u32[]{:S(2)}) async-start(bf16[16,32,3584]{2,1,0:T(8,128)(2,1)} %bitcast.48), calls=%async_computation.1 | async-start | bytes 7340032 | tf_op jit(solution)/shard_map/all_to_all | solution.py:74
  126.3 116.9 %reduce-scatter.2.cloned.1.call-start = ((), (), s32[]{:S(2)}) async-start(), calls=%async_computation.4 | async-start | bytes 3899392 | tf_op jit(solution)/shard_map/reduce_scatter | solution.py:94
  179.7 4.2 %copy-start.2 = (bf16[4,256,576]{1,2,0:T(8,128)(2,1)S(1)}, bf16[4,256,576]{1,2,0:T(8,128)(2,1)}, u32[]{:S(2)}) copy-start(bf16[4,256,576]{1,2,0:T(8,128)(2,1)} %param.11) | copy-start | bytes 3538948
  179.7 4.2 %copy-start.4 = (s32[4]{0:T(128)S(1)}, s32[4]{0:T(128)}, u32[]{:S(2)}) copy-start(s32[4]{0:T(128)} %param.12) | copy-start | bytes 52
Sparse Core Ops, SparseCore 0:
  9.8 42.4 all-gather.3
  183.4 59.8 reduce-scatter.1
where the time goes:
time: 252 us
  waiting for transfers between devices  113 us (45%)
  blocking collectives  86.3 us (34%)
  matrix products  19.4 us (8%)
  between operations  14.9 us (6%)
  other arithmetic  7.63 us (3%)
  starting transfers between devices  7.18 us (3%)
  local copies, waits for them, and re-layouts  3.1 us (1%)
    reduce_scatter x1, waiting for transfers between devices, per_device(): lax.psum_scatter(column_mixed, 'grp', scatter_dimension=0, tiled=True)  57.5 us
    all_to_all x1, blocking collectives, per_device(): lax.all_to_all(doubled, 'ep', split_axis=0, concat_axis=0, tiled=True)  50.4 us
    all_to_all x1, waiting for transfers between devices, per_device(): lax.all_to_all(partials.reshape(peer_count, expert_slots, feature), 'ep',...  33.3 us
    all_gather x1, waiting for transfers between devices, per_device(): all_tokens = lax.all_gather(tokens, 'grp', axis=0, tiled=True)  21.8 us
    all_gather x1, blocking collectives, per_device(): all_ids = lax.all_gather(ids, 'grp', axis=0, tiled=True)  20.4 us
    all_gather x1, blocking collectives, per_device(): all_gates = lax.all_gather(gates, 'grp', axis=0, tiled=True)  15.6 us
    dot_general x1, matrix products, expert_partial(): return jnp.dot(hidden, w_down[0], preferred_element_type=jnp.float32)  10 us
    all_to_all x1, starting transfers between devices, per_device(): lax.all_to_all(partials.reshape(peer_count, expert_slots, feature), 'ep',...  7.11 us
  transfers between devices with their start and end apart: 3, of which 3 were waited for; matrix products, arithmetic and copies ran while one was open for 2% of the time, Pallas kernels for 0%

commit v1 on v0

--- a/solution.py
+++ b/solution.py
@@ -46,7 +46,8 @@
     slot_count = pair_count * expert_slots
     column_rows = group_count * row_count
     all_tokens = lax.all_gather(tokens, "grp", axis=0, tiled=True)
-    all_ids = lax.all_gather(ids, "grp", axis=0, tiled=True)
+    repeated = jnp.stack([ids] * lax.axis_size("grp"))
+    all_ids = jnp.concatenate(lax.all_to_all(repeated, "grp", 0, 0), axis=0)
     all_gates = lax.all_gather(gates, "grp", axis=0, tiled=True)
     my_group = lax.axis_index("grp")
     local = all_ids - pair_count * my_group

time: 252 us -> 252 us (level)
  blocking collectives: 86.3 us -> 66 us
  waiting for transfers between devices: 113 us -> 122 us
  starting transfers between devices: 7.18 us -> 15.7 us
    all_gather x1 -> x0, blocking collectives: 20.4 us -> none  [per_device(): all_ids = lax.all_gather(ids, 'grp', axis=0, tiled=True)]
    all_to_all x0 -> x1, starting transfers between devices: none -> 8.57 us  [per_device(): all_ids = jnp.concatenate(lax.all_to_all(repeated, 'grp', 0, 0), axis=0)]
    all_to_all x0 -> x1, waiting for transfers between devices: none -> 7.47 us  [per_device(): all_ids = jnp.concatenate(lax.all_to_all(repeated, 'grp', 0, 0), axis=0)]
  transfers between devices with their start and end apart: 3 -> 4, of which waited for: 3 -> 4; matrix products, arithmetic and copies ran while one was open for 2% -> 3% of each run, Pallas kernels for 0% -> 0%
where the time goes in v1:
time: 252 us
  waiting for transfers between devices  122 us (48%)
  blocking collectives  66 us (26%)
  matrix products  19.4 us (8%)
  starting transfers between devices  15.7 us (6%)
  between operations  14.9 us (6%)
  other arithmetic  8.3 us (3%)
  local copies, waits for them, and re-layouts  5.07 us (2%)
    reduce_scatter x1, waiting for transfers between devices, per_device(): lax.psum_scatter(column_mixed, 'grp', scatter_dimension=0, tiled=True)  57.5 us
    all_to_all x1, blocking collectives, per_device(): lax.all_to_all(doubled, 'ep', split_axis=0, concat_axis=0, tiled=True)  50.4 us
    all_to_all x1, waiting for transfers between devices, per_device(): lax.all_to_all(partials.reshape(peer_count, expert_slots, feature), 'ep',...  33.3 us
    all_gather x1, waiting for transfers between devices, per_device(): all_tokens = lax.all_gather(tokens, 'grp', axis=0, tiled=True)  23.4 us
    all_gather x1, blocking collectives, per_device(): all_gates = lax.all_gather(gates, 'grp', axis=0, tiled=True)  15.6 us
    dot_general x1, matrix products, expert_partial(): return jnp.dot(hidden, w_down[0], preferred_element_type=jnp.float32)  10.1 us
    all_to_all x1, starting transfers between devices, per_device(): all_ids = jnp.concatenate(lax.all_to_all(repeated, 'grp', 0, 0), axis=0)  8.57 us
    all_to_all x1, waiting for transfers between devices, per_device(): all_ids = jnp.concatenate(lax.all_to_all(repeated, 'grp', 0, 0), axis=0)  7.47 us
  transfers between devices with their start and end apart: 4, of which 4 were waited for; matrix products, arithmetic and copies ran while one was open for 3% of the time, Pallas kernels for 0%

profile of v1, /device:TPU:6, one launch (start us, length us, event | category | flops | bytes accessed | tf_op | source)
XLA Modules:
  0.0 251.8 jit_solution(9392191671633722607)
XLA Ops:
  7.2 0.0 copy-start
  7.2 0.0 all-gather.3.cloned.1.call-start
  7.2 0.7 all-gather.3.cloned.1.call-update
  7.9 0.7 broadcast_bitcast_fusion
  8.6 0.7 reshape.132
  9.3 8.6 %all-to-all-start = ((s32[16,1,128]{2,1,0:T(1,128)}), s32[16,1,128]{2,1,0:T(1,128)S(1)}, u32[]{:S(2)}, u32[]{:S(2)}) async-start(s32[16,1,128]{2,1,0:T(1,128)} %reshape.132), calls=%async_computation | async-start | bytes 16384 | tf_op jit(solution)/shard_map/all_to_all | solution.py:50
  17.9 7.5 %all-to-all-done = s32[16,1,128]{2,1,0:T(1,128)S(1)} async-done(((s32[16,1,128]{2,1,0:T(1,128)}), s32[16,1,128]{2,1,0:T(1,128)S(1)}, u32[]{:S(2)}, u32[]{:S(2)}) %all-to-all-start) | async-done | bytes 8224 | tf_op jit(solution)/shard_map/all_to_all | solution.py:50
  25.4 0.5 broadcast.94
  25.9 0.7 reduce.1
  26.6 0.1 reshape.133
  26.7 0.1 sub.39
  26.8 0.1 reshape.123
  26.9 0.1 copy.37
  27.0 0.7 fusion.30
  27.7 0.1 copy.38
  27.8 0.1 reduce_window_sum.14
  27.9 0.1 add_select_fusion
  28.0 0.1 copy.39
  28.1 0.7 fusion.6
  28.8 23.4 %all-gather.3.cloned.1.call-done = bf16[256,3584]{1,0:T(8,128)(2,1)} async-done(((bf16[16,3584]{1,0:T(8,128)(2,1)}), bf16[256,3584]{1,0:T(8,128)(2,1)}) %all-gather.3.cloned.1.call-update) | async-done | bytes 1835024 | tf_op jit(solution)/shard_map/all_gather | solution.py:48
  52.3 2.2 convolution_convert_fusion.1
  54.5 0.4 broadcast_in_dim.46
  54.8 0.0 copy-start.5
  54.9 50.4 %all_to_all.15 = bf16[16,32,3584]{2,1,0:T(8,128)(2,1)S(1)} all-to-all(bf16[16,32,3584]{2,1,0:T(8,128)(2,1)S(1)} %bitcast.48), channel_id=1, replica_groups=mesh['grp'=16,'ep'=16] {'ep'}, dimensions={0} | all-to-all | bytes 7340032 | tf_op jit(solution)/shard_map/all_to_all | solution.py:71
  105.3 1.8 copy-done.1
  107.1 0.0 copy-done.5
  107.1 2.1 fusion.4
  109.2 10.1 %convolution_convert_fusion = bf16[512,3584]{1,0:T(8,128)(2,1)} fusion(bf16[1,512,3584]{2,1,0:T(8,128)(2,1)} %param.19, bf16[512,3584]{1,0:T(8,128)(2,1)} %bitcast.53, bf16[1,3584,512]{2,1,0:T(8,128)(2,1)} %param.18, f32[512,512]{1,0:T(8,128)S(1)} %fusion.4), kind=kOutput, calls=%fused_computation.1 | convolution fusion | flops 3761504256 | bytes 15728640 | tf_op jit(solution)/shard_map/dot_general | solution.py:35
  119.2 7.1 %all-to-all-start.2 = ((bf16[16,32,3584]{2,1,0:T(8,128)(2,1)}), bf16[16,32,3584]{2,1,0:T(8,128)(2,1)}, u32[]{:S(2)}, u32[]{:S(2)}) async-start(bf16[16,32,3584]{2,1,0:T(8,128)(2,1)} %bitcast.51), calls=%async_computation.2 | async-start | bytes 7340032 | tf_op jit(solution)/shard_map/all_to_all | solution.py:75
  126.3 0.0 reduce-scatter.2.cloned.1.call-start
  126.4 0.0 copy-done.3
  126.4 15.6 %all-gather = f32[16,16,8]{1,2,0:T(8,128)S(1)} all-gather(f32[1,16,8]{1,2,0:T(8,128)S(1)} %bitcast.54), channel_id=1, replica_groups=mesh['grp'=16,'ep'=16] {'grp'}, dimensions={0}, use_global_device_ids=true | all-gather | bytes 8704 | tf_op jit(solution)/shard_map/all_gather | solution.py:51
  141.9 0.1 reshape.131
  142.1 0.1 copy.41
  142.2 1.5 select_reduce_fusion
  143.7 33.3 %all-to-all-done.2 = bf16[16,32,3584]{2,1,0:T(8,128)(2,1)} async-done(((bf16[16,32,3584]{2,1,0:T(8,128)(2,1)}), bf16[16,32,3584]{2,1,0:T(8,128)(2,1)}, u32[]{:S(2)}, u32[]{:S(2)}) %all-to-all-start.2) | async-done | bytes 3670048 | tf_op jit(solution)/shard_map/all_to_all | solution.py:75
  176.9 2.8 %bitcast_reduce_fusion = bf16[8,32,3584]{2,1,0:T(8,128)(2,1)S(1)} fusion(bf16[16,32,3584]{2,1,0:T(8,128)(2,1)} %all-to-all-done.2), kind=kLoop, calls=%fused_computation.3 | loop fusion | flops 917504 | bytes 5505024 | tf_op jit(solution)/shard_map/reduce_sum | solution.py:85
  179.7 0.0 copy-start.2
  179.7 0.0 copy-start.4
  179.7 3.5 %fusion.31 = f32[256,3584]{1,0:T(8,128)} fusion(f32[256,256]{1,0:T(8,128)S(1)} %select_reduce_fusion, bf16[256,3584]{1,0:T(8,128)(2,1)S(1)} %bitcast.50), kind=kOutput, calls=%fused_computation.46 | convolution fusion | flops 2818572288 | bytes 5767168 | tf_op jit(solution)/shard_map/dot_general | solution.py:89
  183.2 0.0 reduce-scatter.2.cloned.1.call-update
  183.9 0.0 copy-done
  183.9 0.0 copy-done.2
  183.9 0.3 fusion.14
  184.3 0.2 fusion.29
  184.5 1.2 fusion.17
  185.8 57.5 %reduce-scatter.2.cloned.1.call-done = f32[16,3584]{1,0:T(8,128)} async-done(((f32[256,3584]{1,0:T(8,128)}), f32[16,3584]{1,0:T(8,128)}) %reduce-scatter.2.cloned.1.call-update) | async-done | bytes 229392 | tf_op jit(solution)/shard_map/reduce_scatter | solution.py:95
  243.3 1.6 convert_element_type.35
  (11 shorter events, 0.1 us)
Async XLA Ops:
  7.2 176.7 %copy-start = (bf16[4,64,576]{2,1,0:T(8,128)(2,1)S(1)}, bf16[4,64,576]{2,1,0:T(8,128)(2,1)}, u32[]{:S(2)}) copy-start(bf16[4,64,576]{2,1,0:T(8,128)(2,1)} %param.10) | copy-start | bytes 884740
  7.2 45.1 %all-gather.3.cloned.1.call-start = ((), (), s32[]{:S(2)}) async-start(), calls=%async_computation.4 | async-start | bytes 1949696 | tf_op jit(solution)/shard_map/all_gather | solution.py:48
  9.3 16.1 %all-to-all-start = ((s32[16,1,128]{2,1,0:T(1,128)}), s32[16,1,128]{2,1,0:T(1,128)S(1)}, u32[]{:S(2)}, u32[]{:S(2)}) async-start(s32[16,1,128]{2,1,0:T(1,128)} %reshape.132), calls=%async_computation | async-start | bytes 16384 | tf_op jit(solution)/shard_map/all_to_all | solution.py:50
  54.8 52.3 %copy-start.5 = (bf16[1,3584,512]{2,1,0:T(8,128)(2,1)S(1)}, bf16[1,3584,512]{2,1,0:T(8,128)(2,1)}, u32[]{:S(2)}) copy-start(bf16[1,3584,512]{2,1,0:T(8,128)(2,1)} %param.17) | copy-start | bytes 11010052
  105.3 1.8 copy-start.1
  119.2 7.2 %copy-start.3 = (f32[16,8]{0,1:T(8,128)S(1)}, f32[16,8]{0,1:T(8,128)}, u32[]{:S(2)}) copy-start(f32[16,8]{0,1:T(8,128)} %param.16) | copy-start | bytes 1540
  119.2 57.7 %all-to-all-start.2 = ((bf16[16,32,3584]{2,1,0:T(8,128)(2,1)}), bf16[16,32,3584]{2,1,0:T(8,128)(2,1)}, u32[]{:S(2)}, u32[]{:S(2)}) async-start(bf16[16,32,3584]{2,1,0:T(8,128)(2,1)} %bitcast.51), calls=%async_computation.2 | async-start | bytes 7340032 | tf_op jit(solution)/shard_map/all_to_all | solution.py:75
  126.3 117.0 %reduce-scatter.2.cloned.1.call-start = ((), (), s32[]{:S(2)}) async-start(), calls=%async_computation.5 | async-start | bytes 3899392 | tf_op jit(solution)/shard_map/reduce_scatter | solution.py:95
  179.7 4.2 %copy-start.2 = (bf16[4,256,576]{1,2,0:T(8,128)(2,1)S(1)}, bf16[4,256,576]{1,2,0:T(8,128)(2,1)}, u32[]{:S(2)}) copy-start(bf16[4,256,576]{1,2,0:T(8,128)(2,1)} %param.11) | copy-start | bytes 3538948
  179.7 4.2 %copy-start.4 = (s32[4]{0:T(128)S(1)}, s32[4]{0:T(128)}, u32[]{:S(2)}) copy-start(s32[4]{0:T(128)} %param.12) | copy-start | bytes 52
Sparse Core Ops, SparseCore 0:
  9.8 42.3 all-gather.2
  183.4 59.9 reduce-scatter.1
